TPU v7x, 256 devices: a whole 4x4x8 slice. The times are simulated.
256 devices in a mesh: shard: 16 (over z, core), tensor: 4 (over x), section: 4 (over y).
Axes of the slice: x: 4, y: 4, z: 8, core: 2. Of those that a mesh axis runs over, the one named last changes fastest.
Arguments:
- gradient: bfloat16 [6, 2048, 8192], P(None, ('tensor', 'section'), 'shard'), may hold values from -6 to 6
- basis: bfloat16 [6, 2048, 256], P(None, ('tensor', 'section')), may hold values from -6 to 6
- moment_m: float32 [6, 8192, 256], P(None, ('shard', 'tensor', 'section')), may hold values from -4 to 4
- moment_v: float32 [6, 8192, 256], P(None, ('shard', 'tensor', 'section')), may hold values from 0.002 to 0.02
Outputs:
- delta: bfloat16 [6, 2048, 8192], P(None, ('tensor', 'section'), 'shard')
- basis_new: bfloat16 [6, 2048, 256], P(None, ('tensor', 'section'))
- moment_m_new: float32 [6, 8192, 256], P(None, ('shard', 'tensor', 'section'))
- moment_v_new: float32 [6, 8192, 256], P(None, ('shard', 'tensor', 'section'))
All inputs are finite; a program needn't handle non-finite values. Where the computation divides by a largest or mean magnitude, that divisor is 1e-20 or more.
Results may differ from a plain program's by a relative error of at most 0.0049.
Values may be sent and summed in bfloat16 or wider, within the bound.
A program may use at most 64 MiB of HBM per device.

v0:
```python
import math
import jax
import jax.numpy as jnp
from jax import lax
from jax.sharding import PartitionSpec as P

D = 2048
NS_ITERS = 4
beta_one = 0.9
beta_two = 0.999
bias_one = 1.0 - 0.9**10
bias_two = 1.0 - 0.999**10
eps_adam = 1e-08
galore_gain = 4.0


def gram_total(iterate):
    local_gram = jnp.einsum("kmr,kms->krs", iterate, iterate, precision=lax.Precision.HIGHEST)
    return lax.psum(local_gram, ("tensor", "section"))


def orthogonal(subspace):
    gram_mat = gram_total(subspace)
    row_bound = jnp.max(jnp.sum(jnp.abs(gram_mat), axis=2), axis=1)[:, None, None] + 1e-06
    iterate = subspace / jnp.sqrt(row_bound)
    gram_mat = gram_mat / row_bound
    identity = jnp.eye(gram_mat.shape[1], dtype=jnp.float32)
    for turn_index in range(NS_ITERS):
        factor = 1.5 * identity - 0.5 * gram_mat
        iterate = jnp.einsum("kmr,krs->kms", iterate, factor, precision=lax.Precision.HIGHEST)
        if turn_index + 1 < NS_ITERS:
            gram_mat = gram_total(iterate)
    return iterate


def per_device(gradient, basis, moment_m, moment_v):
    width_root = math.sqrt(D)
    partial_low = jnp.einsum("kmn,kmr->knr", gradient, basis, preferred_element_type=jnp.float32)
    low_rank = (
        lax.psum_scatter(partial_low, ("tensor", "section"), scatter_dimension=1, tiled=True)
        / width_root
    )
    moment_m_new = beta_one * moment_m + (1.0 - beta_one) * low_rank
    moment_v_new = beta_two * moment_v + (1.0 - beta_two) * low_rank * low_rank
    step_low = (moment_m_new / bias_one / (jnp.sqrt(moment_v_new / bias_two) + eps_adam)).astype(
        jnp.bfloat16
    )
    rough_low = low_rank.astype(jnp.bfloat16)
    step_block, rough_block = (
        lax.all_gather(step_low, ("tensor", "section"), axis=1, tiled=True),
        lax.all_gather(rough_low, ("tensor", "section"), axis=1, tiled=True),
    )
    delta = (
        -galore_gain
        / width_root
        * jnp.einsum("kmr,knr->kmn", basis, step_block, preferred_element_type=jnp.float32)
    ).astype(jnp.bfloat16)
    subspace = jnp.einsum("kmn,knr->kmr", gradient, rough_block, preferred_element_type=jnp.float32)
    whole_sum = lax.psum(subspace, "shard")
    basis_new = (width_root * orthogonal(whole_sum)).astype(jnp.bfloat16)
    return (delta, basis_new, moment_m_new, moment_v_new)


def solution(mesh):
    placed = (
        P(None, ("tensor", "section"), "shard"),
        P(None, ("tensor", "section"), None),
        P(None, ("shard", "tensor", "section"), None),
        P(None, ("shard", "tensor", "section"), None),
    )
    return jax.shard_map(
        per_device,
        mesh=mesh,
        in_specs=placed,
        out_specs=(
            P(None, ("tensor", "section"), "shard"),
            P(None, ("tensor", "section"), None),
            P(None, ("shard", "tensor", "section"), None),
            P(None, ("shard", "tensor", "section"), None),
        ),
        check_vma=False,
    )
```

profile of v0, /device:TPU:32, one launch (start us, length us, event | category | flops | bytes accessed | tf_op | source)
XLA Modules:
  0.0 738.4 jit_solution(1374766177256162602)
XLA Ops:
  7.2 1.1 copy-done
  8.3 3.3 fusion.37
  11.6 84.4 %reduce-scatter.2.cloned.1.call-done = f32[6,32,256]{2,1,0:T(8,128)} async-done(((f32[6,512,256]{2,1,0:T(8,128)}), f32[6,32,256]{2,1,0:T(8,128)}) %reduce-scatter.2.cloned.1.call-update) | async-done | bytes 196624 | tf_op jit(solution)/shard_map/reduce_scatter | solution.py:40
  96.0 1.8 divide_convert_fusion
  97.9 49.2 %all-gather.5.cloned.1.call-done = bf16[6,512,256]{2,1,0:T(8,128)(2,1)} async-done(((bf16[6,32,256]{2,1,0:T(8,128)(2,1)}), bf16[6,512,256]{2,1,0:T(8,128)(2,1)}) %all-gather.5.cloned.1.call-update) | async-done | bytes 1572880 | tf_op jit(solution)/shard_map/all_gather | solution.py:51
  147.2 2.9 convolution_bitcast_fusion
  150.2 108.3 %all-reduce.6.cloned.1.call-done = f32[6,128,256]{1,2,0:T(8,128)} async-done(((f32[6,128,256]{1,2,0:T(8,128)}), f32[6,128,256]{1,2,0:T(8,128)}) %all-reduce.6.cloned.1.call-update) | async-done | bytes 786448 | tf_op jit(solution)/shard_map/psum | solution.py:59
  258.5 3.9 fusion.38
  262.5 102.3 %all-reduce.8.cloned.1.call-done = f32[6,256,256]{2,1,0:T(8,128)} async-done(((f32[6,256,256]{2,1,0:T(8,128)}), f32[6,256,256]{2,1,0:T(8,128)}) %all-reduce.8.cloned.1.call-update) | async-done | bytes 1572880 | tf_op jit(solution)/shard_map/psum | solution.py:19
  364.8 1.7 abs_reduce_fusion
  366.6 3.2 fusion.9
  369.8 2.6 fusion.39
  372.5 98.7 %all-reduce.10.cloned.1.call-done = f32[6,256,256]{2,1,0:T(8,128)} async-done(((f32[6,256,256]{2,1,0:T(8,128)}), f32[6,256,256]{2,1,0:T(8,128)}) %all-reduce.10.cloned.1.call-update) | async-done | bytes 1572880 | tf_op jit(solution)/shard_map/psum | solution.py:19
  471.1 2.6 fusion.6
  473.7 2.6 fusion.40
  476.4 0.7 all-gather.3.cloned.1.call-update
  477.3 97.7 %all-reduce.12.cloned.1.call-done = f32[6,256,256]{2,1,0:T(8,128)} async-done(((f32[6,256,256]{2,1,0:T(8,128)}), f32[6,256,256]{2,1,0:T(8,128)}) %all-reduce.12.cloned.1.call-update) | async-done | bytes 1572880 | tf_op jit(solution)/shard_map/psum | solution.py:19
  575.1 2.6 fusion.3
  577.6 2.6 fusion.41
  580.3 46.1 %all-gather.3.cloned.1.call-done = bf16[6,512,256]{2,1,0:T(8,128)(2,1)} async-done(((bf16[6,32,256]{2,1,0:T(8,128)(2,1)}), bf16[6,512,256]{2,1,0:T(8,128)(2,1)}) %all-gather.3.cloned.1.call-update) | async-done | bytes 1572880 | tf_op jit(solution)/shard_map/all_gather | solution.py:50
  626.4 2.0 fusion.13
  628.3 1.2 copy.15
  629.5 98.7 %all-reduce.14.cloned.1.call-done = f32[6,256,256]{2,1,0:T(8,128)} async-done(((f32[6,256,256]{2,1,0:T(8,128)}), f32[6,256,256]{2,1,0:T(8,128)}) %all-reduce.14.cloned.1.call-update) | async-done | bytes 1572880 | tf_op jit(solution)/shard_map/psum | solution.py:19
  728.2 3.3 fusion.17
  (27 shorter events, 0.8 us)
Async XLA Ops:
  7.2 1.1 copy-start
  7.2 88.8 %reduce-scatter.2.cloned.1.call-start = ((), (), s32[]{:S(2)}) async-start(), calls=%async_computation.1 | async-start | bytes 3342336 | tf_op jit(solution)/shard_map/reduce_scatter | solution.py:40
  11.6 84.4 %copy-start.3 = (f32[6,32,256]{2,1,0:T(8,128)S(1)}, f32[6,32,256]{2,1,0:T(8,128)}, u32[]{:S(2)}) copy-start(f32[6,32,256]{2,1,0:T(8,128)} %param.6) | copy-start | bytes 589828
  11.6 84.4 %copy-start.4 = (f32[6,32,256]{2,1,0:T(8,128)S(1)}, f32[6,32,256]{2,1,0:T(8,128)}, u32[]{:S(2)}) copy-start(f32[6,32,256]{2,1,0:T(8,128)} %param.7) | copy-start | bytes 589828
  11.6 135.6 %all-gather.5.cloned.1.call-start = ((), (), s32[]{:S(2)}) async-start(), calls=%async_computation.3 | async-start | bytes 1671168 | tf_op jit(solution)/shard_map/all_gather | solution.py:51
  97.9 160.6 %all-reduce.6.cloned.1.call-start = ((), (), s32[]{:S(2)}) async-start(), calls=%async_computation.4 | async-start | bytes 1572864 | tf_op jit(solution)/shard_map/psum | solution.py:59
  150.1 214.7 %all-reduce.8.cloned.1.call-start = ((), (), s32[]{:S(2)}) async-start(), calls=%async_computation.5 | async-start | bytes 3145728 | tf_op jit(solution)/shard_map/psum | solution.py:19
  262.4 104.2 %copy-start.1 = (f32[6,128,256]{1,2,0:T(8,128)S(1)}, f32[6,128,256]{1,2,0:T(8,128)}, u32[]{:S(2)}) copy-start(f32[6,128,256]{1,2,0:T(8,128)} %all-reduce.6.cloned.1.call-done) | copy-start | bytes 2359300
  262.5 208.7 %all-reduce.10.cloned.1.call-start = ((), (), s32[]{:S(2)}) async-start(), calls=%async_computation.6 | async-start | bytes 3145728 | tf_op jit(solution)/shard_map/psum | solution.py:19
  372.4 202.6 %all-reduce.12.cloned.1.call-start = ((), (), s32[]{:S(2)}) async-start(), calls=%async_computation.7 | async-start | bytes 3145728 | tf_op jit(solution)/shard_map/psum | solution.py:19
  476.4 150.0 %all-gather.3.cloned.1.call-start = ((), (), s32[]{:S(2)}) async-start(), calls=%async_computation.2 | async-start | bytes 1671168 | tf_op jit(solution)/shard_map/all_gather | solution.py:50
  477.1 251.1 %all-reduce.14.cloned.1.call-start = ((), (), s32[]{:S(2)}) async-start(), calls=%async_computation.8 | async-start | bytes 3145728 | tf_op jit(solution)/shard_map/psum | solution.py:19
  580.3 46.1 %copy-start.2 = (bf16[6,128,256]{2,1,0:T(8,128)(2,1)S(1)}, bf16[6,128,256]{2,1,0:T(8,128)(2,1)}, u32[]{:S(2)}) copy-start(bf16[6,128,256]{2,1,0:T(8,128)(2,1)} %param.5) | copy-start | bytes 1179652
Sparse Core Ops, SparseCore 0:
  11.7 84.2 reduce-scatter.1
  99.1 48.0 all-gather.4
  150.2 108.2 all-reduce.5
  262.6 102.1 all-reduce.7
  372.6 98.5 all-reduce.9
  476.5 98.5 all-reduce.11
  578.1 48.1 all-gather.2
  629.7 98.5 all-reduce.13
where the time goes:
time: 739 us; the launch traced here: 738 us
  waiting for transfers between devices  686 us (93%)
  matrix products  31.6 us (4%)
  between operations  14.2 us (2%)
    psum x4, waiting for transfers between devices, gram_total(): return lax.psum(local_gram, ('tensor', 'section'))  397 us
    psum x1, waiting for transfers between devices, per_device(): whole_sum = lax.psum(subspace, 'shard')  108 us
    reduce_scatter x1, waiting for transfers between devices, per_device(): lax.psum_scatter(partial_low, ('tensor', 'section'), scatter_dimension=1,...  84.4 us
    all_gather x1, waiting for transfers between devices, per_device(): lax.all_gather(rough_low, ('tensor', 'section'), axis=1, tiled=True)  49.2 us
    all_gather x1, waiting for transfers between devices, per_device(): lax.all_gather(step_low, ('tensor', 'section'), axis=1, tiled=True)  46.1 us
  transfers between devices with their start and end apart: 8, of which 8 were waited for; matrix products, arithmetic and copies ran while one was open for 1% of the time, Pallas kernels for 0%

commit v1 on v0

--- a/solution.py
+++ b/solution.py
@@ -12,6 +12,14 @@
 bias_two = 1.0 - 0.999**10
 eps_adam = 1e-08
 galore_gain = 4.0
+
+
+def boxes_replace(target, array_dim):
+    target = jnp.moveaxis(target, 0, array_dim)
+    v_now = target.shape
+    return target.reshape(
+        *v_now[:array_dim], v_now[array_dim] * v_now[array_dim + 1], *v_now[array_dim + 2 :]
+    )
 
 
 def gram_total(iterate):
@@ -46,8 +54,28 @@
         jnp.bfloat16
     )
     rough_low = low_rank.astype(jnp.bfloat16)
+
+    def choose_space(mesh_dim, which_dim, page):
+        size_here = lax.axis_size(mesh_dim)
+        made = [(num, (num + 1) % size_here) for num in range(size_here)]
+        passed, kept_arr = ([], [])
+        j = 0
+        all_blocks = [(nth, q) for q, nth in made]
+        while j < size_here - 1:
+            if j % 2 == 0:
+                passed.append(lax.ppermute(passed[-1] if passed else page, mesh_dim, made))
+            else:
+                kept_arr.append(
+                    lax.ppermute(kept_arr[-1] if kept_arr else page, mesh_dim, all_blocks)
+                )
+            j += 1
+        x_new = jnp.stack([*passed[::-1], page, *kept_arr])
+        o_now = lax.axis_index(mesh_dim) - len(passed)
+        x_new = x_new[(jnp.arange(size_here) - o_now) % size_here]
+        return boxes_replace(x_new, which_dim)
+
     step_block, rough_block = (
-        lax.all_gather(step_low, ("tensor", "section"), axis=1, tiled=True),
+        choose_space(("tensor", "section"), 1, step_low),
         lax.all_gather(rough_low, ("tensor", "section"), axis=1, tiled=True),
     )
     delta = (

time: 739 us -> 692 us (0.936)
  waiting for transfers between devices: 686 us -> 586 us
  starting transfers between devices: 0.51 us -> 39.3 us
  local copies, waits for them, and re-layouts: 2.26 us -> 17.9 us
    psum x4, waiting for transfers between devices: 397 us -> 315 us  [gram_total(): return lax.psum(local_gram, ('tensor', 'section'))]
    all_gather x1 -> x0, waiting for transfers between devices: 46.1 us -> none  [per_device(): lax.all_gather(step_low, ('tensor', 'section'), axis=1, tiled=True)]
    ppermute x0 -> x15, starting transfers between devices: none -> 38.8 us  [the longest x7 37.7 us: choose_space(): lax.ppermute(kept_arr[-1] if kept_arr else page, mesh_dim, all_blocks)]
    ppermute x0 -> x15, waiting for transfers between devices: none -> 29.2 us  [the longest x8 29.2 us: choose_space(): passed.append(lax.ppermute(passed[-1] if passed else page, mesh_dim, made))]
    unnamed x11 -> x34, local copies, waits for them, and re-layouts: 2.26 us -> 14.2 us
  transfers between devices with their start and end apart: 8 -> 22, of which waited for: 8 -> 15; matrix products, arithmetic and copies ran while one was open for 1% -> 4% of each run, Pallas kernels for 0% -> 0%
where the time goes in v1:
time: 692 us
  waiting for transfers between devices  586 us (85%)
  starting transfers between devices  39.3 us (6%)
  matrix products  30.1 us (4%)
  local copies, waits for them, and re-layouts  17.9 us (3%)
  between operations  14.3 us (2%)
    psum x4, waiting for transfers between devices, gram_total(): return lax.psum(local_gram, ('tensor', 'section'))  315 us
    psum x1, waiting for transfers between devices, per_device(): whole_sum = lax.psum(subspace, 'shard')  108 us
    reduce_scatter x1, waiting for transfers between devices, per_device(): lax.psum_scatter(partial_low, ('tensor', 'section'), scatter_dimension=1,...  84.3 us
    all_gather x1, waiting for transfers between devices, per_device(): lax.all_gather(rough_low, ('tensor', 'section'), axis=1, tiled=True)  49.3 us
    ppermute x7, starting transfers between devices, choose_space(): lax.ppermute(kept_arr[-1] if kept_arr else page, mesh_dim, all_blocks)  37.7 us
    ppermute x8, waiting for transfers between devices, choose_space(): passed.append(lax.ppermute(passed[-1] if passed else page, mesh_dim, made))  29.2 us
    unnamed x34, local copies, waits for them, and re-layouts  14.2 us
  transfers between devices with their start and end apart: 22, of which 15 were waited for; matrix products, arithmetic and copies ran while one was open for 4% of the time, Pallas kernels for 0%

profile of v1, /device:TPU:32, one launch (start us, length us, event | category | flops | bytes accessed | tf_op | source)
XLA Modules:
  0.0 691.7 jit_solution(11213821798657025995)
XLA Ops:
  8.3 3.3 fusion.39
  11.6 84.3 %reduce-scatter.2.cloned.1.call-done = f32[6,32,256]{2,1,0:T(8,128)} async-done(((f32[6,512,256]{2,1,0:T(8,128)}), f32[6,32,256]{2,1,0:T(8,128)}) %reduce-scatter.2.cloned.1.call-update) | async-done | bytes 196624 | tf_op jit(solution)/shard_map/reduce_scatter | solution.py:48
  97.9 49.3 %all-gather.2.cloned.1.call-done = bf16[6,512,256]{2,1,0:T(8,128)(2,1)} async-done(((bf16[6,32,256]{2,1,0:T(8,128)(2,1)}), bf16[6,512,256]{2,1,0:T(8,128)(2,1)}) %all-gather.2.cloned.1.call-update) | async-done | bytes 1572880 | tf_op jit(solution)/shard_map/all_gather | solution.py:79
  147.1 2.9 convolution_bitcast_fusion
  150.1 108.3 %all-reduce.6.cloned.1.call-done = f32[6,128,256]{1,2,0:T(8,128)} async-done(((f32[6,128,256]{1,2,0:T(8,128)}), f32[6,128,256]{1,2,0:T(8,128)}) %all-reduce.6.cloned.1.call-update) | async-done | bytes 786448 | tf_op jit(solution)/shard_map/psum | solution.py:87
  258.5 3.9 fusion.40
  262.5 102.3 %all-reduce.8.cloned.1.call-done = f32[6,256,256]{2,1,0:T(8,128)} async-done(((f32[6,256,256]{2,1,0:T(8,128)}), f32[6,256,256]{2,1,0:T(8,128)}) %all-reduce.8.cloned.1.call-update) | async-done | bytes 1572880 | tf_op jit(solution)/shard_map/psum | solution.py:27
  366.6 3.2 fusion.9
  373.5 6.9 collective-permute-done
  380.4 5.3 collective-permute-start.8
  385.8 3.5 collective-permute-done.1
  389.3 5.3 collective-permute-start.9
  394.6 4.6 collective-permute-done.2
  399.2 5.3 collective-permute-start.10
  404.5 3.4 collective-permute-done.3
  408.0 5.3 collective-permute-start.11
  413.3 3.1 collective-permute-done.4
  416.5 5.3 collective-permute-start.12
  424.5 5.4 collective-permute-start.13
  432.4 5.5 collective-permute-start.14
  442.4 31.3 %all-reduce.10.cloned.1.call-done = f32[6,256,256]{2,1,0:T(8,128)} async-done(((f32[6,256,256]{2,1,0:T(8,128)}), f32[6,256,256]{2,1,0:T(8,128)}) %all-reduce.10.cloned.1.call-update) | async-done | bytes 1572880 | tf_op jit(solution)/shard_map/psum | solution.py:27
  484.3 93.4 %all-reduce.12.cloned.1.call-done = f32[6,256,256]{2,1,0:T(8,128)} async-done(((f32[6,256,256]{2,1,0:T(8,128)}), f32[6,256,256]{2,1,0:T(8,128)}) %all-reduce.12.cloned.1.call-update) | async-done | bytes 1572880 | tf_op jit(solution)/shard_map/psum | solution.py:27
  593.3 88.3 %all-reduce.14.cloned.1.call-done = f32[6,256,256]{2,1,0:T(8,128)} async-done(((f32[6,256,256]{2,1,0:T(8,128)}), f32[6,256,256]{2,1,0:T(8,128)}) %all-reduce.14.cloned.1.call-update) | async-done | bytes 1572880 | tf_op jit(solution)/shard_map/psum | solution.py:27
  681.6 3.3 fusion.17
  (82 shorter events, 44.6 us)
Async XLA Ops:
  7.2 88.8 %reduce-scatter.2.cloned.1.call-start = ((), (), s32[]{:S(2)}) async-start(), calls=%async_computation.1 | async-start | bytes 3342336 | tf_op jit(solution)/shard_map/reduce_scatter | solution.py:48
  11.6 84.4 %copy-start.4 = (f32[6,32,256]{2,1,0:T(8,128)S(1)}, f32[6,32,256]{2,1,0:T(8,128)}, u32[]{:S(2)}) copy-start(f32[6,32,256]{2,1,0:T(8,128)} %param.7) | copy-start | bytes 589828
  11.6 135.5 %all-gather.2.cloned.1.call-start = ((), (), s32[]{:S(2)}) async-start(), calls=%async_computation.2 | async-start | bytes 1671168 | tf_op jit(solution)/shard_map/all_gather | solution.py:79
  97.8 160.7 %all-reduce.6.cloned.1.call-start = ((), (), s32[]{:S(2)}) async-start(), calls=%async_computation.3 | async-start | bytes 1572864 | tf_op jit(solution)/shard_map/psum | solution.py:87
  150.1 214.7 %all-reduce.8.cloned.1.call-start = ((), (), s32[]{:S(2)}) async-start(), calls=%async_computation.4 | async-start | bytes 3145728 | tf_op jit(solution)/shard_map/psum | solution.py:27
  262.4 104.2 %copy-start.1 = (f32[6,128,256]{1,2,0:T(8,128)S(1)}, f32[6,128,256]{1,2,0:T(8,128)}, u32[]{:S(2)}) copy-start(f32[6,128,256]{1,2,0:T(8,128)} %all-reduce.6.cloned.1.call-done) | copy-start | bytes 2359300
  262.4 211.4 %all-reduce.10.cloned.1.call-start = ((), (), s32[]{:S(2)}) async-start(), calls=%async_computation.5 | async-start | bytes 3145728 | tf_op jit(solution)/shard_map/psum | solution.py:27
  372.4 205.3 %all-reduce.12.cloned.1.call-start = ((), (), s32[]{:S(2)}) async-start(), calls=%async_computation.6 | async-start | bytes 3145728 | tf_op jit(solution)/shard_map/psum | solution.py:27
  372.4 8.0 %collective-permute-start = (bf16[6,32,256]{2,1,0:T(8,128)(2,1)S(1)}, bf16[6,32,256]{2,1,0:T(8,128)(2,1)S(1)}, u32[]{:S(2)}, u32[]{:S(2)}) collective-permute-start(bf16[6,32,256]{2,1,0:T(8,128)(2,1)S(1)} %get-tuple-element.16), channel_id=1, source_target_pairs={{0,1},{1,2},{2,3},{3,4},{4,5},{5,6},{6,7},{7,8},{8,9},{9,10},{10,1... | collective-permute-start | bytes 294920 | tf_op jit(solution)/shard_map/ppermute | solution.py:66
  380.4 8.9 %collective-permute-start.1 = (bf16[6,32,256]{2,1,0:T(8,128)(2,1)S(1)}, bf16[6,32,256]{2,1,0:T(8,128)(2,1)S(1)}, u32[]{:S(2)}, u32[]{:S(2)}) collective-permute-start(bf16[6,32,256]{2,1,0:T(8,128)(2,1)S(1)} %collective-permute-done), channel_id=1, source_target_pairs={{0,1},{1,2},{2,3},{3,4},{4,5},{5,6},{6,7},{7,8},{8,9},{9,10},{10,1... | collective-permute-start | bytes 294920 | tf_op jit(solution)/shard_map/ppermute | solution.py:66
  380.4 8.9 %collective-permute-start.8 = (bf16[6,32,256]{2,1,0:T(8,128)(2,1)S(1)}, bf16[6,32,256]{2,1,0:T(8,128)(2,1)S(1)}, u32[]{:S(2)}, u32[]{:S(2)}) collective-permute-start(bf16[6,32,256]{2,1,0:T(8,128)(2,1)S(1)} %get-tuple-element.16), channel_id=1, source_target_pairs={{1,0},{2,1},{3,2},{4,3},{5,4},{6,5},{7,6},{8,7},{9,8},{10,9},{11,1... | collective-permute-start | bytes 294920 | tf_op jit(solution)/shard_map/ppermute | solution.py:69
  389.3 9.9 %collective-permute-start.2 = (bf16[6,32,256]{2,1,0:T(8,128)(2,1)S(1)}, bf16[6,32,256]{2,1,0:T(8,128)(2,1)S(1)}, u32[]{:S(2)}, u32[]{:S(2)}) collective-permute-start(bf16[6,32,256]{2,1,0:T(8,128)(2,1)S(1)} %collective-permute-done.1), channel_id=1, source_target_pairs={{0,1},{1,2},{2,3},{3,4},{4,5},{5,6},{6,7},{7,8},{8,9},{9,10},{10,1... | collective-permute-start | bytes 294920 | tf_op jit(solution)/shard_map/ppermute | solution.py:66
  389.3 9.9 %collective-permute-start.9 = (bf16[6,32,256]{2,1,0:T(8,128)(2,1)S(1)}, bf16[6,32,256]{2,1,0:T(8,128)(2,1)S(1)}, u32[]{:S(2)}, u32[]{:S(2)}) collective-permute-start(bf16[6,32,256]{2,1,0:T(8,128)(2,1)S(1)} %collective-permute-done.8), channel_id=1, source_target_pairs={{1,0},{2,1},{3,2},{4,3},{5,4},{6,5},{7,6},{8,7},{9,8},{10,9},{11,1... | collective-permute-start | bytes 294920 | tf_op jit(solution)/shard_map/ppermute | solution.py:69
  399.2 8.8 %collective-permute-start.3 = (bf16[6,32,256]{2,1,0:T(8,128)(2,1)S(1)}, bf16[6,32,256]{2,1,0:T(8,128)(2,1)S(1)}, u32[]{:S(2)}, u32[]{:S(2)}) collective-permute-start(bf16[6,32,256]{2,1,0:T(8,128)(2,1)S(1)} %collective-permute-done.2), channel_id=1, source_target_pairs={{0,1},{1,2},{2,3},{3,4},{4,5},{5,6},{6,7},{7,8},{8,9},{9,10},{10,1... | collective-permute-start | bytes 294920 | tf_op jit(solution)/shard_map/ppermute | solution.py:66
  399.2 8.8 %collective-permute-start.10 = (bf16[6,32,256]{2,1,0:T(8,128)(2,1)S(1)}, bf16[6,32,256]{2,1,0:T(8,128)(2,1)S(1)}, u32[]{:S(2)}, u32[]{:S(2)}) collective-permute-start(bf16[6,32,256]{2,1,0:T(8,128)(2,1)S(1)} %collective-permute-done.9), channel_id=1, source_target_pairs={{1,0},{2,1},{3,2},{4,3},{5,4},{6,5},{7,6},{8,7},{9,8},{10,9},{11,1... | collective-permute-start | bytes 294920 | tf_op jit(solution)/shard_map/ppermute | solution.py:69
  408.0 8.5 %collective-permute-start.4 = (bf16[6,32,256]{2,1,0:T(8,128)(2,1)S(1)}, bf16[6,32,256]{2,1,0:T(8,128)(2,1)S(1)}, u32[]{:S(2)}, u32[]{:S(2)}) collective-permute-start(bf16[6,32,256]{2,1,0:T(8,128)(2,1)S(1)} %collective-permute-done.3), channel_id=1, source_target_pairs={{0,1},{1,2},{2,3},{3,4},{4,5},{5,6},{6,7},{7,8},{8,9},{9,10},{10,1... | collective-permute-start | bytes 294920 | tf_op jit(solution)/shard_map/ppermute | solution.py:66
  408.0 8.5 %collective-permute-start.11 = (bf16[6,32,256]{2,1,0:T(8,128)(2,1)S(1)}, bf16[6,32,256]{2,1,0:T(8,128)(2,1)S(1)}, u32[]{:S(2)}, u32[]{:S(2)}) collective-permute-start(bf16[6,32,256]{2,1,0:T(8,128)(2,1)S(1)} %collective-permute-done.10), channel_id=1, source_target_pairs={{1,0},{2,1},{3,2},{4,3},{5,4},{6,5},{7,6},{8,7},{9,8},{10,9},{11,1... | collective-permute-start | bytes 294920 | tf_op jit(solution)/shard_map/ppermute | solution.py:69
  416.5 8.0 %collective-permute-start.5 = (bf16[6,32,256]{2,1,0:T(8,128)(2,1)S(1)}, bf16[6,32,256]{2,1,0:T(8,128)(2,1)S(1)}, u32[]{:S(2)}, u32[]{:S(2)}) collective-permute-start(bf16[6,32,256]{2,1,0:T(8,128)(2,1)S(1)} %collective-permute-done.4), channel_id=1, source_target_pairs={{0,1},{1,2},{2,3},{3,4},{4,5},{5,6},{6,7},{7,8},{8,9},{9,10},{10,1... | collective-permute-start | bytes 294920 | tf_op jit(solution)/shard_map/ppermute | solution.py:66
  416.5 8.0 %collective-permute-start.12 = (bf16[6,32,256]{2,1,0:T(8,128)(2,1)S(1)}, bf16[6,32,256]{2,1,0:T(8,128)(2,1)S(1)}, u32[]{:S(2)}, u32[]{:S(2)}) collective-permute-start(bf16[6,32,256]{2,1,0:T(8,128)(2,1)S(1)} %collective-permute-done.11), channel_id=1, source_target_pairs={{1,0},{2,1},{3,2},{4,3},{5,4},{6,5},{7,6},{8,7},{9,8},{10,9},{11,1... | collective-permute-start | bytes 294920 | tf_op jit(solution)/shard_map/ppermute | solution.py:69
  424.5 7.9 %collective-permute-start.6 = (bf16[6,32,256]{2,1,0:T(8,128)(2,1)S(1)}, bf16[6,32,256]{2,1,0:T(8,128)(2,1)S(1)}, u32[]{:S(2)}, u32[]{:S(2)}) collective-permute-start(bf16[6,32,256]{2,1,0:T(8,128)(2,1)S(1)} %collective-permute-done.5), channel_id=1, source_target_pairs={{0,1},{1,2},{2,3},{3,4},{4,5},{5,6},{6,7},{7,8},{8,9},{9,10},{10,1... | collective-permute-start | bytes 294920 | tf_op jit(solution)/shard_map/ppermute | solution.py:66
  424.5 7.9 %collective-permute-start.13 = (bf16[6,32,256]{2,1,0:T(8,128)(2,1)S(1)}, bf16[6,32,256]{2,1,0:T(8,128)(2,1)}, u32[]{:S(2)}, u32[]{:S(2)}) collective-permute-start(bf16[6,32,256]{2,1,0:T(8,128)(2,1)S(1)} %collective-permute-done.12), channel_id=1, source_target_pairs={{1,0},{2,1},{3,2},{4,3},{5,4},{6,5},{7,6},{8,7},{9,8},{10,9},{11,1... | collective-permute-start | bytes 294920 | tf_op jit(solution)/shard_map/ppermute | solution.py:69
  432.4 8.1 %collective-permute-start.7 = (bf16[6,32,256]{2,1,0:T(8,128)(2,1)S(1)}, bf16[6,32,256]{2,1,0:T(8,128)(2,1)S(1)}, u32[]{:S(2)}, u32[]{:S(2)}) collective-permute-start(bf16[6,32,256]{2,1,0:T(8,128)(2,1)S(1)} %collective-permute-done.6), channel_id=1, source_target_pairs={{0,1},{1,2},{2,3},{3,4},{4,5},{5,6},{6,7},{7,8},{8,9},{9,10},{10,1... | collective-permute-start | bytes 294920 | tf_op jit(solution)/shard_map/ppermute | solution.py:66
  432.4 154.5 %collective-permute-start.14 = (bf16[6,32,256]{2,1,0:T(8,128)(2,1)}, bf16[6,32,256]{2,1,0:T(8,128)(2,1)}, u32[]{:S(2)}, u32[]{:S(2)}) collective-permute-start(bf16[6,32,256]{2,1,0:T(8,128)(2,1)} %collective-permute-done.13), channel_id=1, source_target_pairs={{1,0},{2,1},{3,2},{4,3},{5,4},{6,5},{7,6},{8,7},{9,8},{10,9},{11,1... | collective-permute-start | bytes 294920 | tf_op jit(solution)/shard_map/ppermute | solution.py:69
  479.0 202.6 %all-reduce.14.cloned.1.call-start = ((), (), s32[]{:S(2)}) async-start(), calls=%async_computation.7 | async-start | bytes 3145728 | tf_op jit(solution)/shard_map/psum | solution.py:27
  (7 other events, 133.4 us)
Sparse Core Ops, SparseCore 0:
  11.7 84.2 reduce-scatter.1
  99.0 48.0 all-gather.1
  150.2 108.2 all-reduce.5
  262.5 102.1 all-reduce.7
  372.5 101.2 all-reduce.9
  479.1 98.5 all-reduce.11
  583.0 98.5 all-reduce.13
